TPU v7x, 32 devices: a whole 2x2x4 slice. The times are simulated.
32 devices in a mesh: tm: 8 (over z, x), rows: 4 (over y, core).
Axes of the slice: x: 2, y: 2, z: 4, core: 2. Of those that a mesh axis runs over, the one named last changes fastest.
Arguments:
- latents: bfloat16 [32, 16, 32, 256], P('tm', 'rows'), may hold values from -6 to 6
- frame_gaps: float32 [32], P('tm'), may hold values from 0.5 to 250
- decay_rates: float32 [2, 256], replicated, may hold values from 0.0011 to 0.05
- input_kernel: bfloat16 [2, 3, 3, 256, 256], replicated, may hold values from -0.125 to 0.125
- output_kernel: bfloat16 [2, 3, 3, 256, 256], replicated, may hold values from -0.125 to 0.125
- feedthrough: float32 [2, 256], replicated, may hold values from -1 to 1
Outputs:
- encoded: bfloat16 [32, 16, 32, 256], P('tm', 'rows')
All inputs are finite; a program needn't handle non-finite values.
Results may differ from a plain program's by a relative error of at most 0.012.
Values may be sent and summed in bfloat16 or wider, within the bound.
A program may use at most 64 MiB of HBM per device.

v0:
```python
import jax
import jax.numpy as jnp
from jax import lax
from jax.sharding import PartitionSpec as P

STACK_COUNT = 2


def extended(cells, sides, width):
    for axis, dim in sides:
        count = lax.axis_size(axis)
        ends = count - 1
        head = lax.slice_in_dim(cells, 0, width, axis=dim)
        tail = lax.slice_in_dim(cells, cells.shape[dim] - width, cells.shape[dim], axis=dim)
        cells = jnp.concatenate(
            [
                lax.ppermute(tail, axis, [(i, (i + 1) % count) for i in range(ends)]),
                cells,
                lax.ppermute(head, axis, [((i + 1) % count, i) for i in range(ends)]),
            ],
            axis=dim,
        )
    return cells


def convolve(inputs, kernel):
    frames, vertical_extent, columns, channels = inputs.shape
    padded = extended(inputs, (("rows", 1),), 1)
    padded = jnp.pad(padded, ((0, 0), (0, 0), (1, 1), (0, 0)))
    summed = jnp.zeros((frames * vertical_extent * columns, kernel.shape[-1]), jnp.float32)
    for row_tap in range(3):
        for col_tap in range(3):
            window = padded[
                :, row_tap : row_tap + vertical_extent, col_tap : col_tap + columns, :
            ].reshape(-1, channels)
            summed = summed + jnp.dot(
                window, kernel[row_tap, col_tap], preferred_element_type=jnp.float32
            )
    return summed.reshape(frames, vertical_extent, columns, -1)


def local_states(driving, decays):

    def advance(carried, pieces):
        driven, factor = pieces
        carried = factor * carried + jnp.sqrt(1.0 - factor * factor) * driven
        return (carried, carried)

    initial = jnp.zeros(driving.shape[1:], jnp.float32)
    _, states = lax.scan(advance, initial, (driving, decays))
    return states


def combine(earlier, latter):
    return (earlier[0] * latter[0], latter[0] * earlier[1] + latter[1])


def carried_in(segment_attenuation, block_state):
    band, columns, channels = block_state.shape
    flat_state = block_state.reshape(1, band * columns, channels)
    flattened_decay = segment_attenuation.reshape(1, 1, channels)
    spread_decay, spread_state = (
        lax.all_to_all(flattened_decay, "tm", split_axis=2, concat_axis=0, tiled=True),
        lax.all_to_all(flat_state, "tm", split_axis=2, concat_axis=0, tiled=True),
    )
    _, inclusive = lax.associative_scan(combine, (spread_decay, spread_state), axis=0)
    exclusive = jnp.concatenate([jnp.zeros_like(inclusive[:1]), inclusive[:-1]], axis=0)
    returned = lax.all_to_all(
        exclusive.astype(jnp.bfloat16), "tm", split_axis=0, concat_axis=2, tiled=True
    ).astype(exclusive.dtype)
    incoming = returned.reshape(band, columns, channels)
    return incoming


def per_device(latents, frame_gaps, decay_rates, input_kernel, output_kernel, feedthrough):
    inputs = latents
    for layer_index in range(STACK_COUNT):
        layer_rates = decay_rates[layer_index]
        decays = jnp.exp(-frame_gaps[:, None] * layer_rates[None, :])
        driving = convolve(inputs, input_kernel[layer_index])
        states = local_states(driving, decays)
        cumulative = jnp.cumprod(decays, axis=0)
        incoming = carried_in(cumulative[-1], states[-1])
        states = states + cumulative[:, None, None, :] * incoming[None]
        rounded_states = states.astype(jnp.bfloat16)
        premix = convolve(rounded_states, output_kernel[layer_index]) + feedthrough[
            layer_index
        ] * inputs.astype(jnp.float32)
        inputs = jax.nn.gelu(premix, approximate=True).astype(jnp.bfloat16)
    return inputs


def solution(mesh):
    in_specs = (P("tm", "rows", None, None), P("tm"), P(), P(), P(), P())
    out_specs = P("tm", "rows", None, None)
    return jax.shard_map(
        per_device, mesh=mesh, in_specs=in_specs, out_specs=out_specs, check_vma=False
    )
```

profile of v0, /device:TPU:1, one launch (start us, length us, event | category | flops | bytes accessed | tf_op | source)
XLA Modules:
  0.0 124.7 jit_solution(17457823050170934931)
XLA Ops:
  0.9 4.5 %collective-permute-start = (bf16[4,1,32,256]{3,2,1,0:T(8,128)(2,1)S(1)}, bf16[4,1,32,256]{3,2,1,0:T(8,128)(2,1)S(1)}, u32[]{:S(2)}, u32[]{:S(2)}) collective-permute-start(bf16[4,1,32,256]{3,2,1,0:T(8,128)(2,1)S(1)} %get-tuple-element.163), channel_id=1, source_target_pairs={{0,1},{1,2},{2,3},{4,5},{5,6},{6,7},{8,9},{9,10},{10,11},{12,13},{... | collective-permute-start | bytes 196616 | tf_op jit(solution)/shard_map/ppermute | solution.py:17
  5.4 1.9 %collective-permute-start.1 = (bf16[4,1,32,256]{3,2,1,0:T(8,128)(2,1)S(1)}, bf16[4,1,32,256]{3,2,1,0:T(8,128)(2,1)S(1)}, u32[]{:S(2)}, u32[]{:S(2)}) collective-permute-start(bf16[4,1,32,256]{3,2,1,0:T(8,128)(2,1)S(1)} %get-tuple-element.164), channel_id=1, source_target_pairs={{1,0},{2,1},{3,2},{5,4},{6,5},{7,6},{9,8},{10,9},{11,10},{13,12},{... | collective-permute-start | bytes 196616 | tf_op jit(solution)/shard_map/ppermute | solution.py:19
  9.7 5.5 %all-to-all-start.1 = ((f32[1,1,256]{1,0,2:T(1,128)}), f32[1,1,256]{1,0,2:T(1,128)S(1)}, u32[]{:S(2)}, u32[]{:S(2)}) async-start(f32[1,1,256]{1,0,2:T(1,128)} %copy.39), calls=%async_computation.1 | async-start | bytes 262144 | tf_op jit(solution)/shard_map/all_to_all | solution.py:63
  15.2 1.8 %slice_bitcast_fusion.1 = (bf16[3,3,256,256]{3,2,1,0:T(8,128)(2,1)S(1)}, bf16[3,3,256,256]{3,2,1,0:T(8,128)(2,1)S(1)}) fusion(bf16[2,3,3,256,256]{4,3,2,1,0:T(8,128)(2,1)} %param.13), kind=kLoop, calls=%fused_computation.47 | loop fusion | bytes 4718592 | tf_op jit(solution)/shard_map/squeeze | solution.py:80
  17.1 4.4 %all-to-all-done.1 = f32[1,1,256]{1,0,2:T(1,128)S(1)} async-done(((f32[1,1,256]{1,0,2:T(1,128)}), f32[1,1,256]{1,0,2:T(1,128)S(1)}, u32[]{:S(2)}, u32[]{:S(2)}) %all-to-all-start.1) | async-done | bytes 1056 | tf_op jit(solution)/shard_map/all_to_all | solution.py:63
  21.4 1.0 reduce
  25.1 1.0 fusion.5
  26.2 4.1 %while.26 = (s32[]{:T(128)}, f32[4,32,256]{2,1,0:T(8,128)S(1)}, f32[4,4,32,256]{3,2,1,0:T(8,128)S(1)}, f32[4,256]{1,0:T(4,128)S(1)}, f32[4,4,32,256]{3,2,1,0:T(8,128)}, /*index=5*/s32[]{:T(128)}, s32[]{:T(128)}) while((s32[]{:T(128)}, f32[4,32,256]{2,1,0:T(8,128)S(1)}, f32[4,4,32,256]{3,2,1,0:T(8,128)S(1)}, ...), condition=%wide.region_1.2_spmd.clone, body=%wide.region_0.1_spmd.clone.sunk | while | flops 131587 | bytes 530527 | solution.py:50
  26.2 1.0 bitcast_dynamic-update-slice_fusion.4
  27.2 1.0 bitcast_dynamic-update-slice_fusion.4
  28.3 1.0 bitcast_dynamic-update-slice_fusion.4
  31.0 3.4 %all-to-all-start = ((f32[1,128,256]{1,0,2:T(1,128)}), f32[1,128,256]{1,0,2:T(1,128)S(1)}, u32[]{:S(2)}, u32[]{:S(2)}) async-start(f32[1,128,256]{1,0,2:T(1,128)} %copy.37), calls=%async_computation | async-start | bytes 262144 | tf_op jit(solution)/shard_map/all_to_all | solution.py:64
  34.5 7.2 %all-to-all-done = f32[1,128,256]{1,0,2:T(1,128)S(1)} async-done(((f32[1,128,256]{1,0,2:T(1,128)}), f32[1,128,256]{1,0,2:T(1,128)S(1)}, u32[]{:S(2)}, u32[]{:S(2)}) %all-to-all-start) | async-done | bytes 131104 | tf_op jit(solution)/shard_map/all_to_all | solution.py:64
  42.9 3.4 %all-to-all-start.2 = ((bf16[8,128,32]{1,2,0:T(8,128)(2,1)}), bf16[8,128,32]{1,2,0:T(8,128)(2,1)S(1)}, u32[]{:S(2)}, u32[]{:S(2)}) async-start(bf16[8,128,32]{1,2,0:T(8,128)(2,1)} %concatenate.59), calls=%async_computation.2 | async-start | bytes 131072 | tf_op jit(solution)/shard_map/all_to_all | solution.py:68
  46.3 2.8 %slice_bitcast_fusion = (bf16[3,3,256,256]{3,2,1,0:T(8,128)(2,1)S(1)}, bf16[3,3,256,256]{3,2,1,0:T(8,128)(2,1)}) fusion(bf16[2,3,3,256,256]{4,3,2,1,0:T(8,128)(2,1)} %param.14), kind=kLoop, calls=%fused_computation.46 | loop fusion | bytes 4718592 | tf_op jit(solution)/shard_map/squeeze | solution.py:86
  49.2 2.8 %all-to-all-done.2 = bf16[8,128,32]{1,2,0:T(8,128)(2,1)S(1)} async-done(((bf16[8,128,32]{1,2,0:T(8,128)(2,1)}), bf16[8,128,32]{1,2,0:T(8,128)(2,1)S(1)}, u32[]{:S(2)}, u32[]{:S(2)}) %all-to-all-start.2) | async-done | bytes 65568 | tf_op jit(solution)/shard_map/all_to_all | solution.py:68
  52.0 1.1 reshape.228
  53.1 1.2 copy.45
  54.4 6.2 %collective-permute-start.2 = (bf16[4,1,32,256]{3,2,1,0:T(8,128)(2,1)S(1)}, bf16[4,1,32,256]{3,2,1,0:T(8,128)(2,1)S(1)}, u32[]{:S(2)}, u32[]{:S(2)}) collective-permute-start(bf16[4,1,32,256]{3,2,1,0:T(8,128)(2,1)S(1)} %get-tuple-element.159), channel_id=1, source_target_pairs={{0,1},{1,2},{2,3},{4,5},{5,6},{6,7},{8,9},{9,10},{10,11},{12,13},{... | collective-permute-start | bytes 196616 | tf_op jit(solution)/shard_map/ppermute | solution.py:17
  60.7 1.9 %collective-permute-start.3 = (bf16[4,1,32,256]{3,2,1,0:T(8,128)(2,1)S(1)}, bf16[4,1,32,256]{3,2,1,0:T(8,128)(2,1)S(1)}, u32[]{:S(2)}, u32[]{:S(2)}) collective-permute-start(bf16[4,1,32,256]{3,2,1,0:T(8,128)(2,1)S(1)} %get-tuple-element.160), channel_id=1, source_target_pairs={{1,0},{2,1},{3,2},{5,4},{6,5},{7,6},{9,8},{10,9},{11,10},{13,12},{... | collective-permute-start | bytes 196616 | tf_op jit(solution)/shard_map/ppermute | solution.py:19
  62.7 3.6 %collective-permute-done.3 = bf16[4,1,32,256]{3,2,1,0:T(8,128)(2,1)S(1)} collective-permute-done((bf16[4,1,32,256]{3,2,1,0:T(8,128)(2,1)S(1)}, bf16[4,1,32,256]{3,2,1,0:T(8,128)(2,1)S(1)}, u32[]{:S(2)}, u32[]{:S(2)}) %collective-permute-start.3) | collective-permute-done | bytes 65568 | tf_op jit(solution)/shard_map/ppermute | solution.py:19
  70.1 1.9 %collective-permute-start.4 = (bf16[4,1,32,256]{3,2,1,0:T(8,128)(2,1)S(1)}, bf16[4,1,32,256]{3,2,1,0:T(8,128)(2,1)S(1)}, u32[]{:S(2)}, u32[]{:S(2)}) collective-permute-start(bf16[4,1,32,256]{3,2,1,0:T(8,128)(2,1)S(1)} %get-tuple-element.155), channel_id=1, source_target_pairs={{0,1},{1,2},{2,3},{4,5},{5,6},{6,7},{8,9},{9,10},{10,11},{12,13},{... | collective-permute-start | bytes 196616 | tf_op jit(solution)/shard_map/ppermute | solution.py:17
  72.0 2.4 %collective-permute-start.5 = (bf16[4,1,32,256]{3,2,1,0:T(8,128)(2,1)S(1)}, bf16[4,1,32,256]{3,2,1,0:T(8,128)(2,1)S(1)}, u32[]{:S(2)}, u32[]{:S(2)}) collective-permute-start(bf16[4,1,32,256]{3,2,1,0:T(8,128)(2,1)S(1)} %get-tuple-element.156), channel_id=1, source_target_pairs={{1,0},{2,1},{3,2},{5,4},{6,5},{7,6},{9,8},{10,9},{11,10},{13,12},{... | collective-permute-start | bytes 196616 | tf_op jit(solution)/shard_map/ppermute | solution.py:19
  75.3 3.4 %all-to-all-start.4 = ((f32[1,1,256]{1,0,2:T(1,128)}), f32[1,1,256]{1,0,2:T(1,128)S(1)}, u32[]{:S(2)}, u32[]{:S(2)}) async-start(f32[1,1,256]{1,0,2:T(1,128)} %copy.43), calls=%async_computation.4 | async-start | bytes 262144 | tf_op jit(solution)/shard_map/all_to_all | solution.py:63
  78.7 7.0 %all-to-all-done.4 = f32[1,1,256]{1,0,2:T(1,128)S(1)} async-done(((f32[1,1,256]{1,0,2:T(1,128)}), f32[1,1,256]{1,0,2:T(1,128)S(1)}, u32[]{:S(2)}, u32[]{:S(2)}) %all-to-all-start.4) | async-done | bytes 1056 | tf_op jit(solution)/shard_map/all_to_all | solution.py:63
  85.7 1.0 reduce.1
  90.9 3.4 %all-to-all-start.3 = ((f32[1,128,256]{1,0,2:T(1,128)}), f32[1,128,256]{1,0,2:T(1,128)S(1)}, u32[]{:S(2)}, u32[]{:S(2)}) async-start(f32[1,128,256]{1,0,2:T(1,128)} %copy.41), calls=%async_computation.3 | async-start | bytes 262144 | tf_op jit(solution)/shard_map/all_to_all | solution.py:64
  94.4 6.1 %all-to-all-done.3 = f32[1,128,256]{1,0,2:T(1,128)S(1)} async-done(((f32[1,128,256]{1,0,2:T(1,128)}), f32[1,128,256]{1,0,2:T(1,128)S(1)}, u32[]{:S(2)}, u32[]{:S(2)}) %all-to-all-start.3) | async-done | bytes 131104 | tf_op jit(solution)/shard_map/all_to_all | solution.py:64
  101.1 8.9 %all_to_all.78 = bf16[8,128,32]{1,2,0:T(8,128)(2,1)S(1)} all-to-all(bf16[8,128,32]{1,2,0:T(8,128)(2,1)S(1)} %concatenate.68), channel_id=1, replica_groups=mesh['tm'=8,'rows'=4] {'tm'}, dimensions={0} | all-to-all | bytes 131072 | tf_op jit(solution)/shard_map/all_to_all | solution.py:68
  110.6 4.9 %collective-permute-start.6 = (bf16[4,1,32,256]{3,2,1,0:T(8,128)(2,1)S(1)}, bf16[4,1,32,256]{3,2,1,0:T(8,128)(2,1)S(1)}, u32[]{:S(2)}, u32[]{:S(2)}) collective-permute-start(bf16[4,1,32,256]{3,2,1,0:T(8,128)(2,1)S(1)} %get-tuple-element.151), channel_id=1, source_target_pairs={{0,1},{1,2},{2,3},{4,5},{5,6},{6,7},{8,9},{9,10},{10,11},{12,13},{... | collective-permute-start | bytes 196616 | tf_op jit(solution)/shard_map/ppermute | solution.py:17
  115.5 1.9 %collective-permute-start.7 = (bf16[4,1,32,256]{3,2,1,0:T(8,128)(2,1)S(1)}, bf16[4,1,32,256]{3,2,1,0:T(8,128)(2,1)S(1)}, u32[]{:S(2)}, u32[]{:S(2)}) collective-permute-start(bf16[4,1,32,256]{3,2,1,0:T(8,128)(2,1)S(1)} %get-tuple-element.152), channel_id=1, source_target_pairs={{1,0},{2,1},{3,2},{5,4},{6,5},{7,6},{9,8},{10,9},{11,10},{13,12},{... | collective-permute-start | bytes 196616 | tf_op jit(solution)/shard_map/ppermute | solution.py:19
  117.5 3.6 %collective-permute-done.7 = bf16[4,1,32,256]{3,2,1,0:T(8,128)(2,1)S(1)} collective-permute-done((bf16[4,1,32,256]{3,2,1,0:T(8,128)(2,1)S(1)}, bf16[4,1,32,256]{3,2,1,0:T(8,128)(2,1)S(1)}, u32[]{:S(2)}, u32[]{:S(2)}) %collective-permute-start.7) | collective-permute-done | bytes 65568 | tf_op jit(solution)/shard_map/ppermute | solution.py:19
  (163 shorter events, 22.7 us)
Async XLA Ops:
  0.9 21.8 %collective-permute-start = (bf16[4,1,32,256]{3,2,1,0:T(8,128)(2,1)S(1)}, bf16[4,1,32,256]{3,2,1,0:T(8,128)(2,1)S(1)}, u32[]{:S(2)}, u32[]{:S(2)}) collective-permute-start(bf16[4,1,32,256]{3,2,1,0:T(8,128)(2,1)S(1)} %get-tuple-element.163), channel_id=1, source_target_pairs={{0,1},{1,2},{2,3},{4,5},{5,6},{6,7},{8,9},{9,10},{10,11},{12,13},{... | collective-permute-start | bytes 196616 | tf_op jit(solution)/shard_map/ppermute | solution.py:17
  5.4 17.2 %collective-permute-start.1 = (bf16[4,1,32,256]{3,2,1,0:T(8,128)(2,1)S(1)}, bf16[4,1,32,256]{3,2,1,0:T(8,128)(2,1)S(1)}, u32[]{:S(2)}, u32[]{:S(2)}) collective-permute-start(bf16[4,1,32,256]{3,2,1,0:T(8,128)(2,1)S(1)} %get-tuple-element.164), channel_id=1, source_target_pairs={{1,0},{2,1},{3,2},{5,4},{6,5},{7,6},{9,8},{10,9},{11,10},{13,12},{... | collective-permute-start | bytes 196616 | tf_op jit(solution)/shard_map/ppermute | solution.py:19
  9.7 11.7 %all-to-all-start.1 = ((f32[1,1,256]{1,0,2:T(1,128)}), f32[1,1,256]{1,0,2:T(1,128)S(1)}, u32[]{:S(2)}, u32[]{:S(2)}) async-start(f32[1,1,256]{1,0,2:T(1,128)} %copy.39), calls=%async_computation.1 | async-start | bytes 262144 | tf_op jit(solution)/shard_map/all_to_all | solution.py:63
  15.2 7.4 %copy-start = (bf16[4,4,32,256]{3,2,1,0:T(8,128)(2,1)S(1)}, bf16[4,4,32,256]{3,2,1,0:T(8,128)(2,1)}, u32[]{:S(2)}) copy-start(bf16[4,4,32,256]{3,2,1,0:T(8,128)(2,1)} %param.10) | copy-start | bytes 786436
  31.0 10.6 %all-to-all-start = ((f32[1,128,256]{1,0,2:T(1,128)}), f32[1,128,256]{1,0,2:T(1,128)S(1)}, u32[]{:S(2)}, u32[]{:S(2)}) async-start(f32[1,128,256]{1,0,2:T(1,128)} %copy.37), calls=%async_computation | async-start | bytes 262144 | tf_op jit(solution)/shard_map/all_to_all | solution.py:64
  42.9 9.1 %all-to-all-start.2 = ((bf16[8,128,32]{1,2,0:T(8,128)(2,1)}), bf16[8,128,32]{1,2,0:T(8,128)(2,1)S(1)}, u32[]{:S(2)}, u32[]{:S(2)}) async-start(bf16[8,128,32]{1,2,0:T(8,128)(2,1)} %concatenate.59), calls=%async_computation.2 | async-start | bytes 131072 | tf_op jit(solution)/shard_map/all_to_all | solution.py:68
  52.0 10.6 %copy-start.2 = (f32[2,256]{1,0:T(2,128)S(1)}, f32[2,256]{1,0:T(2,128)}, u32[]{:S(2)}) copy-start(f32[2,256]{1,0:T(2,128)} %param.15) | copy-start | bytes 6148
  54.4 8.2 %collective-permute-start.2 = (bf16[4,1,32,256]{3,2,1,0:T(8,128)(2,1)S(1)}, bf16[4,1,32,256]{3,2,1,0:T(8,128)(2,1)S(1)}, u32[]{:S(2)}, u32[]{:S(2)}) collective-permute-start(bf16[4,1,32,256]{3,2,1,0:T(8,128)(2,1)S(1)} %get-tuple-element.159), channel_id=1, source_target_pairs={{0,1},{1,2},{2,3},{4,5},{5,6},{6,7},{8,9},{9,10},{10,11},{12,13},{... | collective-permute-start | bytes 196616 | tf_op jit(solution)/shard_map/ppermute | solution.py:17
  60.7 5.6 %collective-permute-start.3 = (bf16[4,1,32,256]{3,2,1,0:T(8,128)(2,1)S(1)}, bf16[4,1,32,256]{3,2,1,0:T(8,128)(2,1)S(1)}, u32[]{:S(2)}, u32[]{:S(2)}) collective-permute-start(bf16[4,1,32,256]{3,2,1,0:T(8,128)(2,1)S(1)} %get-tuple-element.160), channel_id=1, source_target_pairs={{1,0},{2,1},{3,2},{5,4},{6,5},{7,6},{9,8},{10,9},{11,10},{13,12},{... | collective-permute-start | bytes 196616 | tf_op jit(solution)/shard_map/ppermute | solution.py:19
  66.5 1.3 %copy-start.1 = (bf16[3,3,256,256]{3,2,1,0:T(8,128)(2,1)S(1)}, bf16[3,3,256,256]{3,2,1,0:T(8,128)(2,1)}, u32[]{:S(2)}) copy-start(bf16[3,3,256,256]{3,2,1,0:T(8,128)(2,1)} %get-tuple-element.122) | copy-start | bytes 3538948
  70.1 16.8 %collective-permute-start.4 = (bf16[4,1,32,256]{3,2,1,0:T(8,128)(2,1)S(1)}, bf16[4,1,32,256]{3,2,1,0:T(8,128)(2,1)S(1)}, u32[]{:S(2)}, u32[]{:S(2)}) collective-permute-start(bf16[4,1,32,256]{3,2,1,0:T(8,128)(2,1)S(1)} %get-tuple-element.155), channel_id=1, source_target_pairs={{0,1},{1,2},{2,3},{4,5},{5,6},{6,7},{8,9},{9,10},{10,11},{12,13},{... | collective-permute-start | bytes 196616 | tf_op jit(solution)/shard_map/ppermute | solution.py:17
  72.0 14.8 %collective-permute-start.5 = (bf16[4,1,32,256]{3,2,1,0:T(8,128)(2,1)S(1)}, bf16[4,1,32,256]{3,2,1,0:T(8,128)(2,1)S(1)}, u32[]{:S(2)}, u32[]{:S(2)}) collective-permute-start(bf16[4,1,32,256]{3,2,1,0:T(8,128)(2,1)S(1)} %get-tuple-element.156), channel_id=1, source_target_pairs={{1,0},{2,1},{3,2},{5,4},{6,5},{7,6},{9,8},{10,9},{11,10},{13,12},{... | collective-permute-start | bytes 196616 | tf_op jit(solution)/shard_map/ppermute | solution.py:19
  75.3 10.4 %all-to-all-start.4 = ((f32[1,1,256]{1,0,2:T(1,128)}), f32[1,1,256]{1,0,2:T(1,128)S(1)}, u32[]{:S(2)}, u32[]{:S(2)}) async-start(f32[1,1,256]{1,0,2:T(1,128)} %copy.43), calls=%async_computation.4 | async-start | bytes 262144 | tf_op jit(solution)/shard_map/all_to_all | solution.py:63
  90.9 9.6 %all-to-all-start.3 = ((f32[1,128,256]{1,0,2:T(1,128)}), f32[1,128,256]{1,0,2:T(1,128)S(1)}, u32[]{:S(2)}, u32[]{:S(2)}) async-start(f32[1,128,256]{1,0,2:T(1,128)} %copy.41), calls=%async_computation.3 | async-start | bytes 262144 | tf_op jit(solution)/shard_map/all_to_all | solution.py:64
  110.6 6.8 %collective-permute-start.6 = (bf16[4,1,32,256]{3,2,1,0:T(8,128)(2,1)S(1)}, bf16[4,1,32,256]{3,2,1,0:T(8,128)(2,1)S(1)}, u32[]{:S(2)}, u32[]{:S(2)}) collective-permute-start(bf16[4,1,32,256]{3,2,1,0:T(8,128)(2,1)S(1)} %get-tuple-element.151), channel_id=1, source_target_pairs={{0,1},{1,2},{2,3},{4,5},{5,6},{6,7},{8,9},{9,10},{10,11},{12,13},{... | collective-permute-start | bytes 196616 | tf_op jit(solution)/shard_map/ppermute | solution.py:17
  115.5 5.6 %collective-permute-start.7 = (bf16[4,1,32,256]{3,2,1,0:T(8,128)(2,1)S(1)}, bf16[4,1,32,256]{3,2,1,0:T(8,128)(2,1)S(1)}, u32[]{:S(2)}, u32[]{:S(2)}) collective-permute-start(bf16[4,1,32,256]{3,2,1,0:T(8,128)(2,1)S(1)} %get-tuple-element.152), channel_id=1, source_target_pairs={{1,0},{2,1},{3,2},{5,4},{6,5},{7,6},{9,8},{10,9},{11,10},{13,12},{... | collective-permute-start | bytes 196616 | tf_op jit(solution)/shard_map/ppermute | solution.py:19
where the time goes:
time: 126 us; the launch traced here: 125 us
  starting transfers between devices  44.8 us (36%)
  waiting for transfers between devices  34.8 us (28%)
  local copies, waits for them, and re-layouts  15.8 us (13%)
  other arithmetic  10.4 us (8%)
  blocking collectives  8.91 us (7%)
  matrix products  8.88 us (7%)
    ppermute x4, starting transfers between devices, extended(): lax.ppermute(tail, axis, [(i, (i + 1) % count) for i in range(ends)])  17.6 us
    all_to_all x2, waiting for transfers between devices, carried_in(): lax.all_to_all(flat_state, 'tm', split_axis=2, concat_axis=0, tiled=True)  13.4 us
    all_to_all x2, waiting for transfers between devices, carried_in(): lax.all_to_all(flattened_decay, 'tm', split_axis=2, concat_axis=0, tiled=...  11.3 us
    all_to_all x1, blocking collectives, carried_in(): lax.all_to_all(exclusive.astype(jnp.bfloat16), 'tm', split_axis=0, concat...  8.91 us
    all_to_all x2, starting transfers between devices, carried_in(): lax.all_to_all(flattened_decay, 'tm', split_axis=2, concat_axis=0, tiled=...  8.9 us
    dot_general x36, matrix products, convolve(): jnp.dot(window, kernel[row_tap, col_tap], preferred_element_type=jnp.floa...  8.88 us
    ppermute x4, starting transfers between devices, extended(): lax.ppermute(head, axis, [((i + 1) % count, i) for i in range(ends)])  8.17 us
    ppermute x4, waiting for transfers between devices, extended(): lax.ppermute(head, axis, [((i + 1) % count, i) for i in range(ends)])  7.24 us
  transfers between devices with their start and end apart: 13, of which 7 were waited for; matrix products, arithmetic and copies ran while one was open for 8% of the time, Pallas kernels for 0%

commit v1 on v0

v1 whole, which is shorter than its diff:
```python
import functools

import jax
import jax.numpy as jnp
from jax import lax
from jax.experimental import pallas as pl
from jax.experimental.pallas import tpu as pltpu
from jax.sharding import PartitionSpec as P

MESH = pl.DeviceIdType.MESH
F32 = jnp.float32
BF16 = jnp.bfloat16


def gelu(v):
    return 0.5 * v * (1.0 + jnp.tanh(0.7978845608028654 * (v + 0.044715 * (v * v * v))))


def kernel(
    n, bands, base, owners,
    lat, gaps, rates, feed, win, wout,
    out,
    x0, x1, xs, st, halo, wbuf, cums, dec_src, dec_box, fin, inbox, outbox, carry,
    lat_sem, w_sem, halo_send, halo_recv, dec_send, dec_recv, fin_send, fin_recv, car_send, car_recv,
):
    layers = win.shape[0]
    frames, rows, width, chans = lat.shape
    per_row = owners // rows
    share = width // per_row
    me = lax.axis_index("tm")
    band = lax.axis_index("rows")
    has_up = band > 0
    has_down = band < bands - 1
    is_owner = jnp.logical_and(me >= base, me < base + owners)
    my_share = me - base
    interior = list(range(1, rows - 1))
    edge = [0, rows - 1]
    pending = []

    def send(cond, src, dst, ssem, rsem, dev):
        copy = pltpu.make_async_remote_copy(
            src_ref=src, dst_ref=dst, send_sem=ssem, recv_sem=rsem, device_id=dev, device_id_type=MESH
        )
        pl.when(cond)(copy.start)
        pending.append((cond, copy))

    def receive(cond, dst, ssem, rsem, dev):
        copy = pltpu.make_async_remote_copy(
            src_ref=dst, dst_ref=dst, send_sem=ssem, recv_sem=rsem, device_id=dev, device_id_type=MESH
        )
        pl.when(cond)(copy.wait_recv)

    barrier = pltpu.get_barrier_semaphore()
    for step in range(1, n):
        pl.semaphore_signal(barrier, inc=1, device_id={"tm": lax.rem(me + step, n)}, device_id_type=MESH)

    @pl.when(has_up)
    def _():
        pl.semaphore_signal(barrier, inc=1, device_id={"rows": band - 1}, device_id_type=MESH)

    @pl.when(has_down)
    def _():
        pl.semaphore_signal(barrier, inc=1, device_id={"rows": band + 1}, device_id_type=MESH)

    row_copies = [pltpu.make_async_copy(lat.at[:, r], x0.at[r], lat_sem.at[r]) for r in range(rows)]
    for copy in row_copies:
        copy.start()
    w_copies = {}
    for layer in range(layers):
        for which, src in enumerate((win, wout)):
            copy = pltpu.make_async_copy(src.at[layer], wbuf.at[layer, which], w_sem.at[layer, which])
            copy.start()
            w_copies[layer, which] = copy

    decays = []
    for layer in range(layers):
        rate = rates[layer : layer + 1, :]
        factors = [jnp.exp(-gaps[t] * rate) for t in range(frames)]
        total = factors[0]
        cums[layer, 0:1, :] = total
        for t in range(1, frames):
            total = total * factors[t]
            cums[layer, t : t + 1, :] = total
        dec_src[layer : layer + 1, :] = total
        decays.append(factors)

    @pl.when(is_owner)
    def _():
        dec_box[me] = dec_src[...]

    @pl.when(jnp.logical_not(has_up))
    def _():
        for layer in range(layers):
            for which in range(2):
                halo[layer, which, 0] = jnp.zeros(halo.shape[3:], BF16)

    @pl.when(jnp.logical_not(has_down))
    def _():
        for layer in range(layers):
            for which in range(2):
                halo[layer, which, 1] = jnp.zeros(halo.shape[3:], BF16)

    @pl.when(me == 0)
    def _():
        carry[...] = jnp.zeros(carry.shape, BF16)

    pl.semaphore_wait(barrier, n - 1 + has_up.astype(jnp.int32) + has_down.astype(jnp.int32))

    def send_halo(layer, which, top, bottom):
        send(has_up, top, halo.at[layer, which, 1], halo_send.at[layer, which, 0],
             halo_recv.at[layer, which, 1], {"rows": band - 1})
        send(has_down, bottom, halo.at[layer, which, 0], halo_send.at[layer, which, 1],
             halo_recv.at[layer, which, 0], {"rows": band + 1})

    def wait_halo(layer, which):
        receive(has_up, halo.at[layer, which, 0], halo_send.at[layer, which, 0],
                halo_recv.at[layer, which, 0], {"rows": band - 1})
        receive(has_down, halo.at[layer, which, 1], halo_send.at[layer, which, 1],
                halo_recv.at[layer, which, 1], {"rows": band + 1})

    send_halo(0, 0, lat.at[:, 0], lat.at[:, rows - 1])
    for s in range(owners):
        send(jnp.logical_and(me < n - 1, me != base + s), dec_src, dec_box.at[me], dec_send.at[s],
             dec_recv.at[me], {"tm": base + s})

    def conv(x, layer, which, wanted):
        def row(i):
            if i < 0:
                v = halo[layer, which, 0]
            elif i == rows:
                v = halo[layer, which, 1]
            else:
                v = x[i]
            return v.reshape(frames * width, chans)

        lhs = [jnp.concatenate([row(i + a - 1) for i in wanted], axis=0) for a in range(3)]
        lhs = jnp.concatenate(lhs, axis=1)
        parts = []
        for b in range(3):
            rhs = jnp.concatenate([wbuf[layer, which, a, b] for a in range(3)], axis=0)
            parts.append(jnp.dot(lhs, rhs, preferred_element_type=F32))
        size = lhs.shape[0]
        column = lax.rem(lax.broadcasted_iota(jnp.int32, (size, parts[0].shape[1]), 0), width)
        left = jnp.where(column == 0, 0.0, pltpu.roll(parts[0], 1, 0))
        right = jnp.where(column == width - 1, 0.0, pltpu.roll(parts[2], size - 1, 0))
        return (parts[1] + left + right).reshape(len(wanted), frames, width, -1)

    def drive(x, layer, wanted):
        driven = conv(x, layer, 0, wanted)
        for j, r in enumerate(wanted):
            state = None
            for t in range(frames):
                factor = decays[layer][t]
                fresh = jnp.sqrt(1.0 - factor * factor) * driven[j, t]
                state = fresh if state is None else factor * state + fresh
                st[r, t] = state
            for piece in range(per_row):
                s = r * per_row + piece
                part = state[piece * share : (piece + 1) * share].astype(BF16)
                fin[layer, s] = part

                @pl.when(me == base + s)
                def _():
                    inbox[layer, me] = part

                send(jnp.logical_and(me < n - 1, me != base + s), fin.at[layer, s], inbox.at[layer, me],
                     fin_send.at[layer, s], fin_recv.at[layer, me], {"tm": base + s})

    def own(layer):
        total = None
        for k in range(1, n):
            receive(jnp.logical_and(is_owner, me != k - 1), inbox.at[layer, k - 1], fin_send.at[layer, 0],
                    fin_recv.at[layer, k - 1], {"tm": k - 1})
            if layer == 0:
                receive(jnp.logical_and(is_owner, me != k - 1), dec_box.at[k - 1], dec_send.at[0],
                        dec_recv.at[k - 1], {"tm": k - 1})
            last = inbox[layer, k - 1].astype(F32)
            total = last if total is None else dec_box[k - 1, layer : layer + 1, :] * total + last
            outbox[layer, k] = total.astype(BF16)

            @pl.when(jnp.logical_and(is_owner, me == k))
            def _():
                carry[layer, my_share] = outbox[layer, k]

            send(jnp.logical_and(is_owner, me != k), outbox.at[layer, k], carry.at[layer, my_share],
                 car_send.at[layer, k], car_recv.at[layer, my_share], {"tm": k})

    def finish(layer, r):
        pieces = []
        for piece in range(per_row):
            s = r * per_row + piece
            receive(jnp.logical_and(me > 0, me != base + s), carry.at[layer, s], car_send.at[layer, 0],
                    car_recv.at[layer, s], {"tm": base + s})
            pieces.append(carry[layer, s].astype(F32))
        incoming = pieces[0] if per_row == 1 else jnp.concatenate(pieces, axis=0)
        for t in range(frames):
            xs[layer, r, t] = (st[r, t] + cums[layer, t : t + 1, :] * incoming).astype(BF16)

    def mix(x, layer, wanted, put):
        mixed = conv(xs.at[layer], layer, 1, wanted)
        gain = feed[layer : layer + 1, :]
        for j, r in enumerate(wanted):
            skipped = x[r].astype(F32)
            put(r, gelu(mixed[j] + gain * skipped).astype(BF16))

    x = x0
    for copy in row_copies:
        copy.wait()
    for layer in range(layers):
        w_copies[layer, 0].wait()
        drive(x, layer, interior)
        wait_halo(layer, 0)
        drive(x, layer, edge)

        own(layer)

        finish(layer, 0)
        finish(layer, rows - 1)
        send_halo(layer, 1, xs.at[layer, 0], xs.at[layer, rows - 1])
        for r in interior:
            finish(layer, r)
        w_copies[layer, 1].wait()
        if layer == layers - 1:
            def put(r, v):
                out[:, r] = v
        else:
            def put(r, v, layer=layer):
                x1[layer, r] = v
        mix(x, layer, interior, put)
        wait_halo(layer, 1)
        mix(x, layer, edge, put)
        if layer < layers - 1:
            x = x1.at[layer]
            send_halo(layer + 1, 0, x.at[0], x.at[rows - 1])

    for cond, copy in pending:
        pl.when(cond)(copy.wait_send)


def per_device(n, bands, latents, frame_gaps, decay_rates, input_kernel, output_kernel, feedthrough):
    frames, rows, width, chans = latents.shape
    layers = input_kernel.shape[0]
    owners = n // 2
    base = n // 4
    share = rows * width // owners
    any_spec = pl.BlockSpec(memory_space=pl.ANY)
    vmem = pl.BlockSpec(memory_space=pltpu.VMEM)
    dma = pltpu.SemaphoreType.DMA
    return pl.pallas_call(
        functools.partial(kernel, n, bands, base, owners),
        out_shape=jax.ShapeDtypeStruct(latents.shape, BF16),
        in_specs=[any_spec, pl.BlockSpec(memory_space=pltpu.SMEM), vmem, vmem, any_spec, any_spec],
        out_specs=vmem,
        scratch_shapes=[
            pltpu.VMEM((rows, frames, width, chans), BF16),
            pltpu.VMEM((max(layers - 1, 1), rows, frames, width, chans), BF16),
            pltpu.VMEM((layers, rows, frames, width, chans), BF16),
            pltpu.VMEM((rows, frames, width, chans), F32),
            pltpu.VMEM((layers, 2, 2, frames, width, chans), BF16),
            pltpu.VMEM((layers, 2) + input_kernel.shape[1:], BF16),
            pltpu.VMEM((layers, frames, chans), F32),
            pltpu.VMEM((layers, chans), F32),
            pltpu.VMEM((n, layers, chans), F32),
            pltpu.VMEM((layers, owners, share, chans), BF16),
            pltpu.VMEM((layers, n, share, chans), BF16),
            pltpu.VMEM((layers, n, share, chans), BF16),
            pltpu.VMEM((layers, owners, share, chans), BF16),
            dma((rows,)),
            dma((layers, 2)),
            dma((layers, 2, 2)),
            dma((layers, 2, 2)),
            dma((owners,)),
            dma((n,)),
            dma((layers, owners)),
            dma((layers, n)),
            dma((layers, n)),
            dma((layers, owners)),
        ],
        compiler_params=pltpu.CompilerParams(collective_id=0, has_side_effects=True),
    )(latents, frame_gaps, decay_rates, feedthrough, input_kernel, output_kernel)


def solution(mesh):
    in_specs = (P("tm", "rows", None, None), P("tm"), P(), P(), P(), P())
    out_specs = P("tm", "rows", None, None)
    return jax.shard_map(
        functools.partial(per_device, mesh.shape["tm"], mesh.shape["rows"]),
        mesh=mesh, in_specs=in_specs, out_specs=out_specs, check_vma=False,
    )
```

time: 126 us -> 35.3 us (0.28)
  the two profiles are of different devices: /device:TPU:1 before, /device:TPU:9 now
where the time goes in v1:
time: 35.3 us; the launch traced here: 35.1 us
  Pallas kernels  33.5 us (95%)
  local copies, waits for them, and re-layouts  1.67 us (5%)
    pallas_call x1, Pallas kernels, per_device(): pl.pallas_call(functools.partial(kernel, n, bands, base, owners), out_sha...  33.5 us
    unnamed x1, local copies, waits for them, and re-layouts  1.67 us

profile of v1, /device:TPU:9, one launch (start us, length us, event | category | flops | bytes accessed | tf_op | source)
XLA Modules:
  0.0 35.1 jit_solution(9519148573388548265)
XLA Ops:
  0.0 33.5 %shard_map.64 = bf16[4,4,32,256]{3,2,1,0:T(8,128)(2,1)} custom-call(bf16[4,4,32,256]{3,2,1,0:T(8,128)(2,1)} %lat.1, f32[4]{0:T(128)} %gaps.1, f32[2,256]{1,0:T(2,128)} %rates.1, f32[2,256]{1,0:T(2,128)} %feed.1, bf16[2,3,3,256,256]{4,3,2,1,0:T(8,128)(2,1)} %win.1, bf16[2,3,3,256,256]{4,3,2,1,0:T(8,128)(2,1)} %wout.1), custom_call_target="tpu_custom_call" | custom-call | tf_op jit(solution)/shard_map/pallas_call | solution.py:249
  33.5 1.7 %copy.8 = bf16[4,4,32,256]{3,2,1,0:T(8,128)(2,1)} copy(bf16[4,4,32,256]{3,2,1,0:T(8,128)(2,1)} %shard_map.64) | data formatting | bytes 524288

commit v2 on v1

v2 whole, which is shorter than its diff:
```python
import functools

import jax
import jax.numpy as jnp
from jax import lax
from jax.experimental import pallas as pl
from jax.experimental.pallas import tpu as pltpu
from jax.sharding import PartitionSpec as P

MESH = pl.DeviceIdType.MESH
F32 = jnp.float32
BF16 = jnp.bfloat16


def gelu(v):
    return 0.5 * v * (1.0 + jnp.tanh(0.7978845608028654 * (v + 0.044715 * (v * v * v))))


def fold(v):
    half = v.shape[-1] // 2
    return jnp.concatenate([v[..., :half], v[..., half:]], axis=-2)


def unfold(v):
    half = v.shape[-2] // 2
    return jnp.concatenate([v[..., :half, :], v[..., half:, :]], axis=-1)


def kernel(
    n, bands, base, owners,
    lat, gaps, rates, feed, win, wout,
    out,
    x0, x1, xs, xh, st, sth, halo, wbuf, cums, dec_src, dec_box, fin, inbox, outbox, carry, hcarry,
    lat_sem, w_sem, halo_send, halo_recv, dec_send, dec_recv, fin_send, fin_recv, car_send, car_recv,
    hcar_send, hcar_recv,
):
    layers = win.shape[0]
    frames, rows, width, chans = lat.shape
    share = width // owners
    me = lax.axis_index("tm")
    band = lax.axis_index("rows")
    has_up = band > 0
    has_down = band < bands - 1
    is_owner = jnp.logical_and(me >= base, me < base + owners)
    my_share = lax.rem(me + owners * n - base, owners)
    groups = [list(range(1, rows - 1)), [0, rows - 1]]
    sides = [(has_up, lax.rem(band + bands - 1, bands)), (has_down, lax.rem(band + 1, bands))]
    pending = []

    def both(*conds):
        return functools.reduce(jnp.logical_and, conds)

    def send(cond, src, dst, ssem, rsem, dev):
        copy = pltpu.make_async_remote_copy(
            src_ref=src, dst_ref=dst, send_sem=ssem, recv_sem=rsem, device_id=dev, device_id_type=MESH
        )
        pl.when(cond)(copy.start)
        pending.append((cond, copy))

    def receive(cond, dst, ssem, rsem, dev):
        copy = pltpu.make_async_remote_copy(
            src_ref=dst, dst_ref=dst, send_sem=ssem, recv_sem=rsem, device_id=dev, device_id_type=MESH
        )
        pl.when(cond)(copy.wait_recv)

    barrier = pltpu.get_barrier_semaphore()

    def greet(cond, dev):
        @pl.when(cond)
        def _():
            pl.semaphore_signal(barrier, inc=1, device_id=dev, device_id_type=MESH)

    for there, other in sides:
        for s in range(owners):
            greet(there, {"tm": base + s, "rows": other})
        greet(both(there, jnp.logical_not(is_owner)), {"rows": other})
    for k in range(n):
        if base <= k < base + owners:
            greet(me != k, {"tm": k})
        else:
            greet(is_owner, {"tm": k})

    row_copies = [pltpu.make_async_copy(lat.at[:, r], x0.at[r], lat_sem.at[r]) for r in range(rows)]
    for copy in row_copies:
        copy.start()
    w_copies = {}
    for layer in range(layers):
        for which, src in enumerate((win, wout)):
            copy = pltpu.make_async_copy(src.at[layer], wbuf.at[layer, which], w_sem.at[layer, which])
            copy.start()
            w_copies[layer, which] = copy

    decays = []
    for layer in range(layers):
        rate = rates[layer : layer + 1, :]
        factors = [jnp.exp(-gaps[t] * rate) for t in range(frames)]
        total = factors[0]
        cums[layer, 0:1, :] = total
        for t in range(1, frames):
            total = total * factors[t]
            cums[layer, t : t + 1, :] = total
        dec_src[layer : layer + 1, :] = total
        decays.append(factors)

    @pl.when(is_owner)
    def _():
        dec_box[me] = dec_src[...]

    for d, (there, _other) in enumerate(sides):
        @pl.when(jnp.logical_not(there))
        def _():
            for layer in range(layers):
                for which in range(2):
                    halo[layer, which, d] = jnp.zeros(halo.shape[3:], BF16)

        @pl.when(jnp.logical_or(me == 0, jnp.logical_not(there)))
        def _():
            for layer in range(layers):
                hcarry[layer, d] = jnp.zeros(hcarry.shape[2:], BF16)

    @pl.when(me == 0)
    def _():
        carry[...] = jnp.zeros(carry.shape, BF16)

    neighbours = has_up.astype(jnp.int32) + has_down.astype(jnp.int32)
    pl.semaphore_wait(
        barrier, jnp.where(is_owner, n - 1 + neighbours * n, owners + neighbours)
    )

    def send_halo(layer, which, top, bottom):
        for d, (src, (there, other)) in enumerate(zip((top, bottom), sides)):
            send(there, src, halo.at[layer, which, 1 - d], halo_send.at[layer, which, d],
                 halo_recv.at[layer, which, 1 - d], {"rows": other})

    def wait_halo(layer, which):
        for d, (there, other) in enumerate(sides):
            receive(there, halo.at[layer, which, d], halo_send.at[layer, which, d],
                    halo_recv.at[layer, which, d], {"rows": other})

    send_halo(0, 0, lat.at[:, 0], lat.at[:, rows - 1])
    for s in range(owners):
        send(both(me < n - 1, me != base + s), dec_src, dec_box.at[me], dec_send.at[s],
             dec_recv.at[me], {"tm": base + s})

    def conv(x, beyond, weights, wanted):
        def row(i):
            v = beyond(0) if i < 0 else beyond(1) if i == rows else x(i)
            return v.reshape(frames * width, chans)

        lhs = [jnp.concatenate([row(i + a - 1) for i in wanted], axis=0) for a in range(3)]
        lhs = jnp.concatenate(lhs, axis=1)
        parts = []
        for b in range(3):
            rhs = jnp.concatenate([weights(a, b) for a in range(3)], axis=0)
            parts.append(jnp.dot(lhs, rhs, preferred_element_type=F32))
        size = lhs.shape[0]
        column = lax.rem(lax.broadcasted_iota(jnp.int32, (size, parts[0].shape[1]), 0), width)
        left = jnp.where(column == 0, 0.0, pltpu.roll(parts[0], 1, 0))
        right = jnp.where(column == width - 1, 0.0, pltpu.roll(parts[2], size - 1, 0))
        return (parts[1] + left + right).reshape(len(wanted), frames, width, -1)

    def drive(x, layer, g):
        driven = conv(x, lambda d: halo[layer, 0, d], lambda a, b: wbuf[layer, 0, a, b], groups[g])
        for j, r in enumerate(groups[g]):
            state = None
            for t in range(frames):
                factor = decays[layer][t]
                fresh = jnp.sqrt(1.0 - factor * factor) * driven[j, t]
                state = fresh if state is None else factor * state + fresh
                st[r, t] = state
                if g == 1:
                    sth[layer, j, t] = state.astype(BF16)
            for s in range(owners):
                fin[layer, g, s, j] = fold(state[s * share : (s + 1) * share]).astype(BF16)
        for s in range(owners):
            @pl.when(me == base + s)
            def _():
                inbox[layer, g, me] = fin[layer, g, s]

            send(both(me < n - 1, me != base + s), fin.at[layer, g, s], inbox.at[layer, g, me],
                 fin_send.at[layer, g, s], fin_recv.at[layer, g, me], {"tm": base + s})
        if g == 1:
            send_halo(layer, 1, sth.at[layer, 0], sth.at[layer, 1])

    def own(layer, g):
        total = None
        for k in range(1, n):
            other = both(is_owner, me != k - 1)
            receive(other, inbox.at[layer, g, k - 1], fin_send.at[layer, g, 0],
                    fin_recv.at[layer, g, k - 1], {"tm": k - 1})
            if layer == 0 and g == 0:
                receive(other, dec_box.at[k - 1], dec_send.at[0], dec_recv.at[k - 1], {"tm": k - 1})
            last = unfold(inbox[layer, g, k - 1].astype(F32))
            total = last if total is None else dec_box[k - 1, layer : layer + 1, :] * total + last
            outbox[layer, g, k] = fold(total).astype(BF16)

            if g == 1:
                for d, (there, band_to) in enumerate(sides):
                    send(both(is_owner, there), outbox.at[layer, g, k, d], hcarry.at[layer, 1 - d, my_share],
                         hcar_send.at[layer, d, k], hcar_recv.at[layer, 1 - d, my_share],
                         {"tm": k, "rows": band_to})
            send(both(is_owner, me != k), outbox.at[layer, g, k], carry.at[layer, g, my_share],
                 car_send.at[layer, g, k], car_recv.at[layer, g, my_share], {"tm": k})

            @pl.when(both(is_owner, me == k))
            def _():
                carry[layer, g, my_share] = outbox[layer, g, k]

    def finish(layer, g):
        for s in range(owners):
            receive(both(me > 0, me != base + s), carry.at[layer, g, s], car_send.at[layer, g, 0],
                    car_recv.at[layer, g, s], {"tm": base + s})
        for j, r in enumerate(groups[g]):
            incoming = jnp.concatenate([unfold(carry[layer, g, s, j].astype(F32)) for s in range(owners)], axis=0)
            for t in range(frames):
                xs[layer, r, t] = (st[r, t] + cums[layer, t : t + 1, :] * incoming).astype(BF16)

    def finish_halo(layer):
        wait_halo(layer, 1)
        for d, (there, band_to) in enumerate(sides):
            for s in range(owners):
                receive(both(me > 0, there), hcarry.at[layer, d, s], hcar_send.at[layer, d, 0],
                        hcar_recv.at[layer, d, s], {"tm": base + s, "rows": band_to})
            incoming = jnp.concatenate([unfold(hcarry[layer, d, s].astype(F32)) for s in range(owners)], axis=0)
            for t in range(frames):
                local = halo[layer, 1, d, t].astype(F32)
                xh[layer, d, t] = (local + cums[layer, t : t + 1, :] * incoming).astype(BF16)

    def mix(x, layer, wanted, put):
        mixed = conv(lambda r: xs[layer, r], lambda d: xh[layer, d], lambda a, b: wbuf[layer, 1, a, b], wanted)
        gain = feed[layer : layer + 1, :]
        for j, r in enumerate(wanted):
            skipped = x(r).astype(F32)
            put(r, gelu(mixed[j] + gain * skipped).astype(BF16))

    x = lambda r: x0[r]
    for copy in row_copies:
        copy.wait()
    for layer in range(layers):
        w_copies[layer, 0].wait()
        drive(x, layer, 0)
        wait_halo(layer, 0)
        drive(x, layer, 1)
        for g in range(2):
            own(layer, g)
        for g in range(2):
            finish(layer, g)
        finish_halo(layer)
        w_copies[layer, 1].wait()
        if layer == layers - 1:
            def put(r, v):
                out[:, r] = v

            mix(x, layer, list(range(rows)), put)
        else:
            def put(r, v):
                x1[layer, r] = v

            mix(x, layer, groups[1], put)
            send_halo(layer + 1, 0, x1.at[layer, 0], x1.at[layer, rows - 1])
            mix(x, layer, groups[0], put)
            x = functools.partial(lambda layer, r: x1[layer, r], layer)

    for cond, copy in pending:
        pl.when(cond)(copy.wait_send)


def per_device(n, bands, latents, frame_gaps, decay_rates, input_kernel, output_kernel, feedthrough):
    frames, rows, width, chans = latents.shape
    layers = input_kernel.shape[0]
    owners = min(n // 2, max(width // 8, 1))
    base = n // 2 - owners // 2
    share = width // owners
    most = max(rows - 2, 2)
    any_spec = pl.BlockSpec(memory_space=pl.ANY)
    vmem = pl.BlockSpec(memory_space=pltpu.VMEM)
    dma = pltpu.SemaphoreType.DMA
    return pl.pallas_call(
        functools.partial(kernel, n, bands, base, owners),
        out_shape=jax.ShapeDtypeStruct(latents.shape, BF16),
        in_specs=[any_spec, pl.BlockSpec(memory_space=pltpu.SMEM), vmem, vmem, any_spec, any_spec],
        out_specs=vmem,
        scratch_shapes=[
            pltpu.VMEM((rows, frames, width, chans), BF16),
            pltpu.VMEM((max(layers - 1, 1), rows, frames, width, chans), BF16),
            pltpu.VMEM((layers, rows, frames, width, chans), BF16),
            pltpu.VMEM((layers, 2, frames, width, chans), BF16),
            pltpu.VMEM((rows, frames, width, chans), F32),
            pltpu.VMEM((layers, 2, frames, width, chans), BF16),
            pltpu.VMEM((layers, 2, 2, frames, width, chans), BF16),
            pltpu.VMEM((layers, 2) + input_kernel.shape[1:], BF16),
            pltpu.VMEM((layers, frames, chans), F32),
            pltpu.VMEM((layers, chans), F32),
            pltpu.VMEM((n, layers, chans), F32),
            pltpu.VMEM((layers, 2, owners, most, 2 * share, chans // 2), BF16),
            pltpu.VMEM((layers, 2, n, most, 2 * share, chans // 2), BF16),
            pltpu.VMEM((layers, 2, n, most, 2 * share, chans // 2), BF16),
            pltpu.VMEM((layers, 2, owners, most, 2 * share, chans // 2), BF16),
            pltpu.VMEM((layers, 2, owners, 2 * share, chans // 2), BF16),
            dma((rows,)),
            dma((layers, 2)),
            dma((layers, 2, 2)),
            dma((layers, 2, 2)),
            dma((owners,)),
            dma((n,)),
            dma((layers, 2, owners)),
            dma((layers, 2, n)),
            dma((layers, 2, n)),
            dma((layers, 2, owners)),
            dma((layers, 2, n)),
            dma((layers, 2, owners)),
        ],
        compiler_params=pltpu.CompilerParams(collective_id=0, has_side_effects=True),
    )(latents, frame_gaps, decay_rates, feedthrough, input_kernel, output_kernel)


def solution(mesh):
    in_specs = (P("tm", "rows", None, None), P("tm"), P(), P(), P(), P())
    out_specs = P("tm", "rows", None, None)
    return jax.shard_map(
        functools.partial(per_device, mesh.shape["tm"], mesh.shape["rows"]),
        mesh=mesh, in_specs=in_specs, out_specs=out_specs, check_vma=False,
    )
```

time: 35.3 us -> 30.3 us (0.86)
  Pallas kernels: 33.5 us -> 28.2 us
    pallas_call x1, Pallas kernels: 33.5 us -> 28.2 us  [per_device(): pl.pallas_call(functools.partial(kernel, n, bands, base, owners), out_sha...]
where the time goes in v2:
time: 30.3 us; the launch traced here: 29.9 us
  Pallas kernels  28.2 us (93%)
  local copies, waits for them, and re-layouts  1.67 us (6%)
    pallas_call x1, Pallas kernels, per_device(): pl.pallas_call(functools.partial(kernel, n, bands, base, owners), out_sha...  28.2 us
    unnamed x1, local copies, waits for them, and re-layouts  1.67 us

profile of v2, /device:TPU:9, one launch (start us, length us, event | category | flops | bytes accessed | tf_op | source)
XLA Modules:
  0.0 29.9 jit_solution(4407954819725085746)
XLA Ops:
  0.0 28.2 %shard_map.64 = bf16[4,4,32,256]{3,2,1,0:T(8,128)(2,1)} custom-call(bf16[4,4,32,256]{3,2,1,0:T(8,128)(2,1)} %lat.1, f32[4]{0:T(128)} %gaps.1, f32[2,256]{1,0:T(2,128)} %rates.1, f32[2,256]{1,0:T(2,128)} %feed.1, bf16[2,3,3,256,256]{4,3,2,1,0:T(8,128)(2,1)} %win.1, bf16[2,3,3,256,256]{4,3,2,1,0:T(8,128)(2,1)} %wout.1), custom_call_target="tpu_custom_call" | custom-call | tf_op jit(solution)/shard_map/pallas_call | solution.py:278
  28.2 1.7 %copy.8 = bf16[4,4,32,256]{3,2,1,0:T(8,128)(2,1)} copy(bf16[4,4,32,256]{3,2,1,0:T(8,128)(2,1)} %shard_map.64) | data formatting | bytes 524288

commit v3 on v2

--- a/solution.py
+++ b/solution.py
@@ -272,12 +272,12 @@
     base = n // 2 - owners // 2
     share = width // owners
     most = max(rows - 2, 2)
-    any_spec = pl.BlockSpec(memory_space=pl.ANY)
+    any_spec = pl.BlockSpec(memory_space=pltpu.HBM)
     vmem = pl.BlockSpec(memory_space=pltpu.VMEM)
     dma = pltpu.SemaphoreType.DMA
     return pl.pallas_call(
         functools.partial(kernel, n, bands, base, owners),
-        out_shape=jax.ShapeDtypeStruct(latents.shape, BF16),
+        out_shape=pltpu.VMEM(latents.shape, BF16),
         in_specs=[any_spec, pl.BlockSpec(memory_space=pltpu.SMEM), vmem, vmem, any_spec, any_spec],
         out_specs=vmem,
         scratch_shapes=[
@@ -310,7 +310,7 @@
             dma((layers, 2, n)),
             dma((layers, 2, owners)),
         ],
-        compiler_params=pltpu.CompilerParams(collective_id=0, has_side_effects=True),
+        compiler_params=pltpu.CompilerParams(collective_id=0, has_side_effects=True, vmem_limit_bytes=60 * 1024 * 1024),
     )(latents, frame_gaps, decay_rates, feedthrough, input_kernel, output_kernel)
 
 

time: 30.3 us -> 28.7 us (0.947)
  local copies, waits for them, and re-layouts: 1.67 us -> 0.71 us
  Pallas kernels: 28.2 us -> 27.5 us
    unnamed x1, local copies, waits for them, and re-layouts: 1.67 us -> 0.71 us
    pallas_call x1, Pallas kernels: 28.2 us -> 27.5 us  [per_device(): pl.pallas_call(functools.partial(kernel, n, bands, base, owners), out_sha...]
where the time goes in v3:
time: 28.7 us; the launch traced here: 28.2 us
  Pallas kernels  27.5 us (96%)
  local copies, waits for them, and re-layouts  0.71 us (2%)
    pallas_call x1, Pallas kernels, per_device(): pl.pallas_call(functools.partial(kernel, n, bands, base, owners), out_sha...  27.5 us
    unnamed x1, local copies, waits for them, and re-layouts  0.71 us

profile of v3, /device:TPU:9, one launch (start us, length us, event | category | flops | bytes accessed | tf_op | source)
XLA Modules:
  0.0 28.2 jit_solution(2684919596398751426)
XLA Ops:
  0.0 27.5 %shard_map.64 = bf16[4,4,32,256]{3,2,1,0:T(8,128)(2,1)S(1)} custom-call(bf16[4,4,32,256]{3,2,1,0:T(8,128)(2,1)} %lat.1, f32[4]{0:T(128)} %gaps.1, f32[2,256]{1,0:T(2,128)} %rates.1, f32[2,256]{1,0:T(2,128)} %feed.1, bf16[2,3,3,256,256]{4,3,2,1,0:T(8,128)(2,1)} %win.1, bf16[2,3,3,256,256]{4,3,2,1,0:T(8,128)(2,1)} %wout.1), custom_call_target="tpu_custom_call" | custom-call | tf_op jit(solution)/shard_map/pallas_call | solution.py:278
  27.5 0.7 %copy.8 = bf16[4,4,32,256]{3,2,1,0:T(8,128)(2,1)} copy(bf16[4,4,32,256]{3,2,1,0:T(8,128)(2,1)S(1)} %shard_map.64) | data formatting | bytes 524288
